TPU v7x, 512 devices: a whole 4x8x8 slice. The times are simulated.
512 devices in a mesh: req: 64 (over z_lo, x, y), tp: 8 (over z_hi, core).
Axes of the slice: x: 4, y: 8, z: 8 (z_hi: 4, z_lo: 2; z = z_hi * 2 + z_lo), core: 2. Of those that a mesh axis runs over, the one named last changes fastest.
Arguments:
- q_proj: bfloat16 [64, 128, 3072], P('req', None, 'tp'), may hold values from -24 to 24, as said below
- kv_proj: bfloat16 [64, 128, 2, 1024], P('req', None, None, 'tp'), may hold values from -6 to 6
- q_bias: bfloat16 [3072], P('tp'), may hold values from -3 to 3
- kv_bias: bfloat16 [2, 1024], P(None, 'tp'), may hold values from -3 to 3
- prefix_kv: bfloat16 [64, 1024, 2, 1024], P('req', None, None, 'tp'), may hold values from -24 to 24, as said below
- lengths: int32 [64], P('req'), may hold values from 1 to 128, 4096 in all
- group_of: int32 [64], P('req'), may hold values from 0 to 2
- owner: int32 [3], replicated, may hold values from 0 to 63
- positions: int32 [64, 128], P('req'), may hold values from 1024 to 1278, as said below
- residual: bfloat16 [64, 128, 5120], P('req', None, 'tp'), may hold values from -6 to 6
- out_weight: bfloat16 [3072, 5120], P(None, 'tp'), may hold values from -0.109375 to 0.109375
Outputs:
- hidden: bfloat16 [64, 128, 5120], P('req', None, 'tp')
Inputs may be any that keep to these rules, and one draw needn't show every extreme that they name: `q_proj`: projected queries; entries stay within the stated bounds. `prefix_kv`: cached keys are already rotated at prefix positions 0 to 1023. Each request's positions are a start of 1024 or more plus the slot index.
All inputs are finite; a program needn't handle non-finite values. No bound on the sum of `lengths` on one device may be relied on, other than what follows from the above.
Results may differ from a plain program's by a relative error of at most 0.006.
Values may be sent and summed in bfloat16 or wider, within the bound.
No kernel may reach another device: no remote copies, remote signals or barrier semaphores. Data moves between devices by JAX's collectives and lax.ppermute only.
A program may use at most 128 MiB of HBM per device.

v0:
```python
import math
import jax
import jax.numpy as jnp
from jax import lax
from jax.sharding import PartitionSpec as P

HD = 128


def spread(x, axis, root):
    mine = lax.axis_index(axis) == root
    return lax.psum(jnp.where(mine, x, jnp.zeros_like(x)), axis)


def rotate(vectors, places):
    half = HD // 2
    index = jnp.arange(half).astype(jnp.float32)
    freqs = jnp.exp(index * (-2.0 / HD) * math.log(1000000.0))
    angles = places.astype(jnp.float32)[:, None] * freqs[None, :]
    cosine = jnp.concatenate([jnp.cos(angles), jnp.cos(angles)], axis=-1)[:, None, :]
    sine = jnp.concatenate([jnp.sin(angles), jnp.sin(angles)], axis=-1)[:, None, :]
    turned = jnp.concatenate([-vectors[..., half:], vectors[..., :half]], axis=-1)
    return vectors * cosine + turned * sine


def attend_rows(queries, all_keys, all_vals, length, prefix_len):
    count = queries.shape[0]
    slots = jnp.arange(count)
    causal = slots[None, :] <= slots[:, None]
    allowed = jnp.concatenate([jnp.ones((count, prefix_len), dtype=bool), causal], axis=1)
    scores = jnp.einsum("rhd,kd->hrk", queries, all_keys, preferred_element_type=jnp.float32) * (
        1.0 / math.sqrt(HD)
    )
    scores = jnp.where(allowed[None], scores, -1e30)
    top = jnp.max(scores, axis=-1, keepdims=True)
    weights = jnp.where(allowed[None], jnp.exp(scores - top), 0.0)
    total = jnp.sum(weights, axis=-1)
    rounded = weights.astype(jnp.bfloat16)
    mixed = jnp.einsum("hrk,kd->rhd", rounded, all_vals, preferred_element_type=jnp.float32)
    mixed = mixed / jnp.transpose(total)[:, :, None]
    mixed = jnp.where((slots < length)[:, None, None], mixed, 0.0)
    return mixed.astype(jnp.bfloat16)


def body(
    q_proj,
    kv_proj,
    q_bias,
    kv_bias,
    prefix_kv,
    lengths,
    group_of,
    owner,
    positions,
    residual,
    out_weight,
):
    cap = q_proj.shape[1]
    prefix_len = prefix_kv.shape[1]
    mine = group_of[0]
    length = lengths[0]
    places = positions[0]
    queries = q_proj[0].astype(jnp.float32).reshape(cap, -1, HD) + q_bias.astype(
        jnp.float32
    ).reshape(-1, HD)
    queries = rotate(queries, places).astype(jnp.bfloat16)
    pairs = kv_proj[0].astype(jnp.float32) + kv_bias.astype(jnp.float32)
    keys = rotate(pairs[:, 0][:, None, :], places)[:, 0].astype(jnp.bfloat16)
    vals = pairs[:, 1].astype(jnp.bfloat16)
    slab = jnp.zeros_like(prefix_kv[0])
    for group in range(owner.shape[0]):
        received = spread(prefix_kv[0], "req", owner[group])
        slab = jnp.where(mine == group, received, slab)
    all_keys = jnp.concatenate([slab[:, 0], keys], axis=0)
    all_vals = jnp.concatenate([slab[:, 1], vals], axis=0)
    attended = attend_rows(queries, all_keys, all_vals, length, prefix_len)
    attended = attended.reshape(cap, -1)
    whole_heads = lax.all_gather(attended, "tp", axis=1, tiled=True)
    projected = jnp.dot(whole_heads, out_weight, preferred_element_type=jnp.float32)
    hidden = (residual[0].astype(jnp.float32) + projected).astype(jnp.bfloat16)
    return hidden[None]


def solution(mesh):
    in_specs = (
        P("req", None, "tp"),
        P("req", None, None, "tp"),
        P("tp"),
        P(None, "tp"),
        P("req", None, None, "tp"),
        P("req"),
        P("req"),
        P(),
        P("req", None),
        P("req", None, "tp"),
        P(None, "tp"),
    )
    out_specs = P("req", None, "tp")
    return jax.shard_map(body, mesh=mesh, in_specs=in_specs, out_specs=out_specs, check_vma=False)
```

profile of v0, /device:TPU:1, one launch (start us, length us, event | category | flops | bytes accessed | tf_op | source)
XLA Modules:
  0.0 664.5 jit_solution(9709575429134257465)
XLA Ops:
  6.5 0.0 all-reduce.4.cloned.1.call-start
  6.5 1.4 fusion.31
  9.9 0.0 copy-start.4
  9.9 0.0 copy-start.1
  9.9 2.3 select_bitcast_fusion
  12.2 0.0 copy-start.5
  12.2 0.0 copy-start.2
  12.2 0.0 copy-start.3
  12.2 0.0 all-reduce.4.cloned.1.call-update
  12.9 0.0 copy-done.4
  12.9 0.3 fusion.22
  13.3 0.1 pad_maximum_fusion
  13.4 0.1 copy.24
  13.5 0.1 copy.25
  13.6 0.0 copy-done.1
  13.6 0.1 copy.23
  13.7 0.0 copy-done.5
  14.4 0.0 copy-done.2
  14.5 0.0 copy-done.3
  14.5 0.1 slice_negate_fusion.1
  14.6 0.1 fusion.21
  14.7 0.1 convert_add_fusion
  14.9 0.1 fusion.17
  15.0 570.6 %all-reduce.4.cloned.1.call-done = (bf16[1024,2,128]{2,0,1:T(8,128)(2,1)}, bf16[1024,2,128]{2,0,1:T(8,128)(2,1)}, bf16[1024,2,128]{2,0,1:T(8,128)(2,1)}) async-done(((bf16[1024,2,128]{2,0,1:T(8,128)(2,1)}, bf16[1024,2,128]{2,0,1:T(8,128)(2,1)}, bf16[1024,2,128]{2,0,1:T(8,128)(2,1)}), (bf16[1024,2,128]{2,0,1:T(8,128)(2,1)}, bf16[1024,2,128]{2,0,1:T(8,128)(2,1)}, ...) | async-done | bytes 1572880 | tf_op jit(solution)/shard_map/psum | solution.py:12
  585.6 1.1 select_select_fusion
  586.7 0.9 fusion.32
  587.7 0.4 fusion.3
  588.1 0.0 copy-start
  588.1 0.6 fusion.10
  588.7 65.4 %all_gather.3 = bf16[128,3072]{0,1:T(8,128)(2,1)S(1)} all-gather(bf16[128,384]{0,1:T(8,128)(2,1)S(1)} %bitcast.78), channel_id=1, replica_groups=mesh['req'=64,'tp'=8] {'tp'}, dimensions={1}, use_global_device_ids=true | all-gather | bytes 884736 | tf_op jit(solution)/shard_map/all_gather | solution.py:78
  654.0 0.0 copy-done
  654.0 3.6 fusion.9
  (11 shorter events, 0.2 us)
Async XLA Ops:
  6.5 579.0 %all-reduce.4.cloned.1.call-start = ((), (), s32[]{:S(2)}) async-start(), calls=%async_computation | async-start | bytes 3145728 | tf_op jit(solution)/shard_map/psum | solution.py:12
  9.9 3.1 copy-start.4
  9.9 3.7 copy-start.1
  12.2 1.5 copy-start.5
  12.2 2.2 copy-start.2
  12.2 2.3 copy-start.3
  588.1 65.9 %copy-start = (bf16[1,128,640]{2,1,0:T(8,128)(2,1)S(1)}, bf16[1,128,640]{2,1,0:T(8,128)(2,1)}, u32[]{:S(2)}) copy-start(bf16[1,128,640]{2,1,0:T(8,128)(2,1)} %param.20) | copy-start | bytes 491524
Sparse Core Ops, SparseCore 0:
  12.4 573.1 all-reduce.3
where the time goes:
time: 665 us; the launch traced here: 664 us
  waiting for transfers between devices  571 us (86%)
  blocking collectives  65.4 us (10%)
  between operations  16.8 us (3%)
    psum x1, waiting for transfers between devices, spread(): return lax.psum(jnp.where(mine, x, jnp.zeros_like(x)), axis)  571 us
    all_gather x1, blocking collectives, body(): whole_heads = lax.all_gather(attended, 'tp', axis=1, tiled=True)  65.4 us
  transfers between devices with their start and end apart: 1, of which 1 were waited for; matrix products, arithmetic and copies ran while one was open for 0% of the time, Pallas kernels for 0%

commit v1 on v0

--- a/solution.py
+++ b/solution.py
@@ -9,7 +9,7 @@
 
 def spread(x, axis, root):
     mine = lax.axis_index(axis) == root
-    return lax.psum(jnp.where(mine, x, jnp.zeros_like(x)), axis)
+    return jnp.sum(lax.all_gather(jnp.where(mine, x, jnp.zeros_like(x)), axis), axis=0)
 
 
 def rotate(vectors, places):

time: 665 us -> 1200 us (1.80)
  waiting for transfers between devices: 571 us -> 1110 us
  blocking collectives: 65.4 us -> 26 us
  other arithmetic: 4.34 us -> 37.3 us
    all_gather x0 -> x3, waiting for transfers between devices: none -> 1110 us  [spread(): lax.all_gather(jnp.where(mine, x, jnp.zeros_like(x)), axis)]
    psum x1 -> x0, waiting for transfers between devices: 571 us -> none  [spread(): return lax.psum(jnp.where(mine, x, jnp.zeros_like(x)), axis)]
    all_gather x1, blocking collectives: 65.4 us -> 26 us  [body(): whole_heads = lax.all_gather(attended, 'tp', axis=1, tiled=True)]
    reduce_sum x0 -> x3, other arithmetic: none -> 34.1 us  [spread(): jnp.sum(lax.all_gather(jnp.where(mine, x, jnp.zeros_like(x)), axis), axis=0)]
  transfers between devices with their start and end apart: 1 -> 3, of which waited for: 1 -> 3; matrix products, arithmetic and copies ran while one was open for 0% -> 2% of each run, Pallas kernels for 0% -> 0%
where the time goes in v1:
time: 1200 us
  waiting for transfers between devices  1110 us (92%)
  other arithmetic  37.3 us (3%)
  blocking collectives  26 us (2%)
  between operations  16.5 us (1%)
    all_gather x3, waiting for transfers between devices, spread(): lax.all_gather(jnp.where(mine, x, jnp.zeros_like(x)), axis)  1110 us
    reduce_sum x3, other arithmetic, spread(): jnp.sum(lax.all_gather(jnp.where(mine, x, jnp.zeros_like(x)), axis), axis=0)  34.1 us
    all_gather x1, blocking collectives, body(): whole_heads = lax.all_gather(attended, 'tp', axis=1, tiled=True)  26 us
  transfers between devices with their start and end apart: 3, of which 3 were waited for; matrix products, arithmetic and copies ran while one was open for 2% of the time, Pallas kernels for 0%

profile of v1, /device:TPU:1, one launch (start us, length us, event | category | flops | bytes accessed | tf_op | source)
XLA Modules:
  0.0 1197.5 jit_solution(7919726225042141972)
XLA Ops:
  6.5 0.0 all-gather.4.cloned.1.call-start
  6.5 1.4 fusion.31
  9.7 0.0 copy-start.4
  9.7 0.0 copy-start.1
  9.8 2.3 broadcast_select_fusion
  12.0 0.0 copy-start.5
  12.0 0.0 copy-start.3
  12.0 0.0 copy-start.2
  12.0 0.0 all-gather.4.cloned.1.call-update
  12.1 0.0 all-gather.6.cloned.1.call-start
  12.1 0.7 all-gather.6.cloned.1.call-update
  12.8 0.0 all-gather.8.cloned.1.call-start
  12.9 0.7 all-gather.8.cloned.1.call-update
  14.2 0.0 copy-done.4
  14.2 0.3 fusion.22
  14.5 0.1 pad_maximum_fusion
  14.7 0.1 copy.34
  14.7 0.1 copy.35
  14.9 0.0 copy-done.1
  14.9 0.1 copy.33
  15.0 0.0 copy-done.5
  15.7 0.0 copy-done.3
  15.8 0.0 copy-done.2
  15.8 0.1 slice_negate_fusion.1
  15.9 0.1 fusion.21
  16.0 0.1 convert_add_fusion
  16.2 0.1 fusion.17
  16.3 375.7 %all-gather.4.cloned.1.call-done = bf16[64,1024,2,128]{3,1,2,0:T(8,128)(2,1)} async-done(((bf16[1,1024,2,128]{3,1,2,0:T(8,128)(2,1)}), bf16[64,1024,2,128]{3,1,2,0:T(8,128)(2,1)}) %all-gather.4.cloned.1.call-update) | async-done | bytes 33554448 | tf_op jit(solution)/shard_map/all_gather | solution.py:12
  392.0 11.4 reduce_sum.45
  403.4 366.3 %all-gather.6.cloned.1.call-done = bf16[64,1024,2,128]{3,1,2,0:T(8,128)(2,1)} async-done(((bf16[1,1024,2,128]{3,1,2,0:T(8,128)(2,1)}), bf16[64,1024,2,128]{3,1,2,0:T(8,128)(2,1)}) %all-gather.6.cloned.1.call-update) | async-done | bytes 33554448 | tf_op jit(solution)/shard_map/all_gather | solution.py:12
  769.7 11.4 reduce_sum.46
  781.1 366.9 %all-gather.8.cloned.1.call-done = bf16[64,1024,2,128]{3,1,2,0:T(8,128)(2,1)} async-done(((bf16[1,1024,2,128]{3,1,2,0:T(8,128)(2,1)}), bf16[64,1024,2,128]{3,1,2,0:T(8,128)(2,1)}) %all-gather.8.cloned.1.call-update) | async-done | bytes 33554448 | tf_op jit(solution)/shard_map/all_gather | solution.py:12
  1147.9 11.4 reduce_sum.47
  1159.3 0.1 select_select_fusion
  1159.4 0.9 fusion.32
  1160.3 0.4 fusion.3
  1160.8 0.0 copy-start
  1160.8 0.6 fusion.10
  1161.3 26.0 %all_gather.18 = bf16[128,3072]{0,1:T(8,128)(2,1)S(1)} all-gather(bf16[128,384]{0,1:T(8,128)(2,1)S(1)} %bitcast.72), channel_id=1, replica_groups=mesh['req'=64,'tp'=8] {'tp'}, dimensions={1}, use_global_device_ids=true | all-gather | bytes 884736 | tf_op jit(solution)/shard_map/all_gather | solution.py:78
  1187.3 0.0 copy-done
  1187.3 3.6 fusion.9
  (11 shorter events, 0.2 us)
Async XLA Ops:
  6.5 385.5 %all-gather.4.cloned.1.call-start = ((), (), s32[]{:S(2)}) async-start(), calls=%async_computation | async-start | bytes 34078720 | tf_op jit(solution)/shard_map/all_gather | solution.py:12
  9.7 4.5 copy-start.4
  9.7 5.1 copy-start.1
  12.0 3.0 copy-start.5
  12.0 3.7 copy-start.3
  12.0 3.7 copy-start.2
  12.1 757.6 %all-gather.6.cloned.1.call-start = ((), (), s32[]{:S(2)}) async-start(), calls=%async_computation.1 | async-start | bytes 34078720 | tf_op jit(solution)/shard_map/all_gather | solution.py:12
  12.8 1135.1 %all-gather.8.cloned.1.call-start = ((), (), s32[]{:S(2)}) async-start(), calls=%async_computation.2 | async-start | bytes 34078720 | tf_op jit(solution)/shard_map/all_gather | solution.py:12
  1160.8 26.6 %copy-start = (bf16[1,128,640]{2,1,0:T(8,128)(2,1)S(1)}, bf16[1,128,640]{2,1,0:T(8,128)(2,1)}, u32[]{:S(2)}) copy-start(bf16[1,128,640]{2,1,0:T(8,128)(2,1)} %param.20) | copy-start | bytes 491524
Sparse Core Ops, SparseCore 0:
  12.2 379.7 all-gather.3
  394.1 375.5 all-gather.5
  771.8 376.0 all-gather.7
